TPU v7x, 32 devices: a whole 2x2x4 slice. The times are simulated.
32 devices in a mesh: shard: 8 (over z, x), rep: 4 (over y, core).
Axes of the slice: x: 2, y: 2, z: 4, core: 2. Of those that a mesh axis runs over, the one named last changes fastest.
Arguments:
- tokens_in: float32 [31520, 768], P(('shard', 'rep')), may hold values from -6 to 6
- routes: int32 [31520, 2], P(('shard', 'rep')), may hold values from 0 to 3, all different within a row; in each aligned block of 985 rows (0 to 984, 985 to 1969, ...) at most 616 rows name the same one
- first_gain: bfloat16 [768], P('shard'), may hold values from 0.5 to 1.5
- first_shift: bfloat16 [768], P('shard'), may hold values from -3 to 3
- joint_weight: bfloat16 [768, 2304], P('shard'), may hold values from -0.21875 to 0.21875
- joint_bias: bfloat16 [2, 768], P(None, 'shard'), may hold values from -3 to 3
- mixer_weight: bfloat16 [768, 768], P('shard'), may hold values from -0.625 to 0.625
- mixer_bias: bfloat16 [768], P('shard'), may hold values from -3 to 3
- second_gain: bfloat16 [768], P('shard'), may hold values from 0.5 to 1.5
- second_shift: bfloat16 [768], P('shard'), may hold values from -3 to 3
- router_weight: bfloat16 [768, 4], P('shard'), may hold values from -0.4375 to 0.4375
- expert_up: bfloat16 [4, 768, 3072], P(None, None, 'shard'), may hold values from -0.21875 to 0.21875
- upward_bias: bfloat16 [4, 3072], P(None, 'shard'), may hold values from -3 to 3
- expert_down: bfloat16 [4, 3072, 768], P(None, 'shard'), may hold values from -0.3125 to 0.3125
- downward_bias: bfloat16 [4, 768], P(None, 'shard'), may hold values from -3 to 3
- out_grad: float32 [31520, 768], P(('shard', 'rep')), may hold values from -6 to 6
Outputs:
- block_out: float32 [31520, 768], P(('shard', 'rep'))
- input_grad: float32 [31520, 768], P(('shard', 'rep'))
- first_gain_grad: float32 [768], P('shard')
- first_shift_grad: float32 [768], P('shard')
- joint_weight_grad: float32 [768, 2304], P('shard')
- joint_bias_grad: float32 [2, 768], P(None, 'shard')
- mixer_weight_grad: float32 [768, 768], P('shard')
- mixer_bias_grad: float32 [768], P('shard')
- second_gain_grad: float32 [768], P('shard')
- second_shift_grad: float32 [768], P('shard')
- router_weight_grad: float32 [768, 4], P('shard')
- expert_up_grad: float32 [4, 768, 3072], P(None, None, 'shard')
- upward_bias_grad: float32 [4, 3072], P(None, 'shard')
- expert_down_grad: float32 [4, 3072, 768], P(None, 'shard')
- downward_bias_grad: float32 [4, 768], P(None, 'shard')
Inputs may be any that keep to these rules, and one draw needn't show every extreme that they name: `routes`: the two experts of a token differ. Among the rows of one device (985 aligned rows), no expert is named more than 616 times.
All inputs are finite; a program needn't handle non-finite values.
Results may differ from a plain program's by a relative error of at most 0.02.
Values may be sent and summed in bfloat16 or wider, within the bound.
A program may use at most 320 MiB of HBM per device.

v0:
```python
import jax
import jax.numpy as jnp
from jax import lax
from jax.sharding import PartitionSpec as P

HEADS = 12
HEAD_DIM = 64
SEQ = 197
CAP = 616


epsilon = 1e-06


def layer_norm(values, gain, shift):
    centre = jnp.mean(values, axis=-1, keepdims=True)
    centred = values - centre
    spread = jnp.mean(centred * centred, axis=-1, keepdims=True)
    factor = lax.rsqrt(spread + epsilon)
    unit_rows = centred * factor
    return (unit_rows * gain + shift, unit_rows, factor)


def norm_back(upstream, unit_rows, factor, gain):
    scaled = upstream * gain
    middle = jnp.mean(scaled, axis=-1, keepdims=True)
    along = jnp.mean(scaled * unit_rows, axis=-1, keepdims=True)
    return factor * (scaled - middle - unit_rows * along)


def gelu_slope(hidden):
    normal_cdf = 0.5 * (1.0 + lax.erf(hidden * 0.7071067811865476))
    density = jnp.exp(-0.5 * hidden * hidden) * 0.3989422804014327
    return normal_cdf + hidden * density


def contract_first(left_rows, right_rows):
    return lax.dot_general(
        left_rows, right_rows, (((0,), (0,)), ((), ())), preferred_element_type=jnp.float32
    )


def contract_last(left_rows, right_rows):
    return lax.dot_general(
        left_rows, right_rows, (((1,), (1,)), ((), ())), preferred_element_type=jnp.float32
    )


def dispatch_tables(routes, experts, capacity):
    token_count = routes.shape[0]
    flat_routes = routes.reshape(-1)
    hit_table = (flat_routes[:, None] == jnp.arange(experts, dtype=jnp.int32)[None, :]).astype(
        jnp.int32
    )
    earlier = jnp.cumsum(hit_table, axis=0) - hit_table
    slot_index = jnp.sum(earlier * hit_table, axis=1)
    position = flat_routes * capacity + slot_index
    entries = jnp.arange(2 * token_count, dtype=jnp.int32)
    owner = jnp.full((experts * capacity,), 2 * token_count, jnp.int32).at[position].set(entries)
    return (position, owner)


def shards(
    tokens_in,
    routes,
    first_gain,
    first_shift,
    joint_weight,
    joint_bias,
    mixer_weight,
    mixer_bias,
    second_gain,
    second_shift,
    router_weight,
    expert_up,
    upward_bias,
    expert_down,
    downward_bias,
    out_grad,
):
    token_count, width = tokens_in.shape
    experts = expert_up.shape[0]
    images = token_count // SEQ
    capacity = CAP
    head_scale = HEAD_DIM ** (-0.5)
    gathered = (
        lax.all_gather(first_gain, "shard", axis=0, tiled=True),
        lax.all_gather(first_shift, "shard", axis=0, tiled=True),
        lax.all_gather(joint_weight, "shard", axis=0, tiled=True),
        lax.all_gather(joint_bias, "shard", axis=1, tiled=True),
        lax.all_gather(mixer_weight, "shard", axis=0, tiled=True),
        lax.all_gather(mixer_bias, "shard", axis=0, tiled=True),
        lax.all_gather(second_gain, "shard", axis=0, tiled=True),
        lax.all_gather(second_shift, "shard", axis=0, tiled=True),
        lax.all_gather(router_weight, "shard", axis=0, tiled=True),
        lax.all_gather(downward_bias, "shard", axis=1, tiled=True),
    )
    (
        gain_one,
        shift_one,
        joint_full,
        joint_shift,
        mixer_full,
        mixer_shift,
        gain_two,
        shift_two,
        router_full,
        down_shift,
    ) = gathered
    gain_one = gain_one.astype(jnp.float32)
    gain_two = gain_two.astype(jnp.float32)
    down_shift = down_shift.astype(jnp.float32)
    normed_one, unit_one, factor_one = layer_norm(
        tokens_in, gain_one, shift_one.astype(jnp.float32)
    )
    normed_one = normed_one.astype(jnp.bfloat16)
    joint_shift = joint_shift.astype(jnp.float32)
    shift_all = jnp.concatenate([joint_shift[0], jnp.zeros((width,), jnp.float32), joint_shift[1]])
    projected = (
        jnp.dot(normed_one, joint_full, preferred_element_type=jnp.float32) + shift_all
    ).astype(jnp.bfloat16)
    parted = projected.reshape(images, SEQ, 3, HEADS, HEAD_DIM)
    queries = parted[:, :, 0]
    key_rows = parted[:, :, 1]
    value_rows = parted[:, :, 2]
    scores = (
        jnp.einsum("bqhd,bkhd->bhqk", queries, key_rows, preferred_element_type=jnp.float32)
        * head_scale
    )
    highest_score = jnp.max(scores, axis=-1, keepdims=True)
    log_total = highest_score + jnp.log(
        jnp.sum(jnp.exp(scores - highest_score), axis=-1, keepdims=True)
    )
    attention = jnp.exp(scores - log_total).astype(jnp.bfloat16)
    mixed = jnp.einsum("bhqk,bkhd->bqhd", attention, value_rows, preferred_element_type=jnp.float32)
    mixed = mixed.reshape(token_count, width).astype(jnp.bfloat16)
    residual_one = tokens_in + (
        jnp.dot(mixed, mixer_full, preferred_element_type=jnp.float32)
        + mixer_shift.astype(jnp.float32)
    )
    normed_two, unit_two, factor_two = layer_norm(
        residual_one, gain_two, shift_two.astype(jnp.float32)
    )
    normed_two = normed_two.astype(jnp.bfloat16)
    logits = jnp.dot(normed_two, router_full, preferred_element_type=jnp.float32)
    router_probs = jax.nn.softmax(logits, axis=-1)
    position, owner = dispatch_tables(routes, experts, capacity)
    choose = (routes[:, :, None] == jnp.arange(experts, dtype=jnp.int32)[None, None, :]).astype(
        jnp.float32
    )
    gates = jnp.sum(choose * router_probs[:, None, :], axis=-1)
    padded = jnp.concatenate([normed_two, jnp.zeros((1, width), jnp.bfloat16)], axis=0)
    dispatched = padded[owner // 2].reshape(experts, capacity, width)
    up_full, up_shift, down_full = (
        lax.all_gather(expert_up, "shard", axis=2, tiled=True),
        lax.all_gather(upward_bias, "shard", axis=1, tiled=True),
        lax.all_gather(expert_down, "shard", axis=1, tiled=True),
    )
    hidden = (
        jnp.einsum("ecd,edf->ecf", dispatched, up_full, preferred_element_type=jnp.float32)
        + up_shift.astype(jnp.float32)[:, None, :]
    )
    active = jax.nn.gelu(hidden, approximate=False).astype(jnp.bfloat16)
    expert_result = (
        jnp.einsum("ecf,efd->ecd", active, down_full, preferred_element_type=jnp.float32)
        + down_shift[:, None, :]
    )
    picked = expert_result.reshape(experts * capacity, width)[position].reshape(
        token_count, 2, width
    )
    block_out = residual_one + jnp.sum(gates[:, :, None] * picked, axis=1)
    gate_pad = jnp.concatenate([gates.reshape(-1), jnp.zeros((1,), jnp.float32)])
    grad_pad = jnp.concatenate([out_grad, jnp.zeros((1, width), jnp.float32)], axis=0)
    result_grad = (
        (gate_pad[owner][:, None] * grad_pad[owner // 2])
        .astype(jnp.bfloat16)
        .reshape(experts, capacity, width)
    )
    gate_grad = jnp.sum(out_grad[:, None, :] * picked, axis=-1)
    probs_grad = jnp.sum(choose * gate_grad[:, :, None], axis=1)
    logit_grad = (
        router_probs * (probs_grad - jnp.sum(router_probs * probs_grad, axis=-1, keepdims=True))
    ).astype(jnp.bfloat16)
    router_grad = contract_first(normed_two, logit_grad)
    normed_grad = contract_last(logit_grad, router_full)
    down_shift_grad = jnp.sum(result_grad.astype(jnp.float32), axis=1)
    up_full, down_full = (
        lax.all_gather(expert_up, "shard", axis=2, tiled=True),
        lax.all_gather(expert_down, "shard", axis=1, tiled=True),
    )
    active_grad = jnp.einsum(
        "ecd,efd->ecf", result_grad, down_full, preferred_element_type=jnp.float32
    )
    hidden_grad = (active_grad * gelu_slope(hidden)).astype(jnp.bfloat16)
    dispatched_grad = jnp.einsum(
        "ecf,edf->ecd", hidden_grad, up_full, preferred_element_type=jnp.float32
    )
    up_grad = jnp.einsum(
        "ecd,ecf->edf", dispatched, hidden_grad, preferred_element_type=jnp.float32
    )
    up_shift_grad = jnp.sum(hidden_grad.astype(jnp.float32), axis=1)
    down_grad = jnp.einsum("ecf,ecd->efd", active, result_grad, preferred_element_type=jnp.float32)
    up_grad, up_shift_grad, down_grad = (
        lax.psum_scatter(
            up_grad.astype(jnp.bfloat16), "shard", scatter_dimension=2, tiled=True
        ).astype(jnp.float32),
        lax.psum_scatter(
            up_shift_grad.astype(jnp.bfloat16), "shard", scatter_dimension=1, tiled=True
        ).astype(jnp.float32),
        lax.psum_scatter(
            down_grad.astype(jnp.bfloat16), "shard", scatter_dimension=1, tiled=True
        ).astype(jnp.float32),
    )
    routed_grad = dispatched_grad.reshape(experts * capacity, width)[position].reshape(
        token_count, 2, width
    )
    normed_grad = normed_grad + jnp.sum(routed_grad, axis=1)
    gain_two_grad = jnp.sum(normed_grad * unit_two, axis=0)
    shift_two_grad = jnp.sum(normed_grad, axis=0)
    residual_grad = out_grad + norm_back(normed_grad, unit_two, factor_two, gain_two)
    mixer_in_grad = residual_grad.astype(jnp.bfloat16)
    mixer_shift_grad = jnp.sum(mixer_in_grad.astype(jnp.float32), axis=0)
    joint_full, mixer_full = (
        lax.all_gather(joint_weight, "shard", axis=0, tiled=True),
        lax.all_gather(mixer_weight, "shard", axis=0, tiled=True),
    )
    mixer_grad = contract_first(mixed, mixer_in_grad)
    mixed_grad = (
        contract_last(mixer_in_grad, mixer_full)
        .astype(jnp.bfloat16)
        .reshape(images, SEQ, HEADS, HEAD_DIM)
    )
    scores_again = (
        jnp.einsum("bqhd,bkhd->bhqk", queries, key_rows, preferred_element_type=jnp.float32)
        * head_scale
    )
    attention_full = jnp.exp(scores_again - log_total)
    attention_low = attention_full.astype(jnp.bfloat16)
    weight_grad = jnp.einsum(
        "bqhd,bkhd->bhqk", mixed_grad, value_rows, preferred_element_type=jnp.float32
    )
    centre_grad = jnp.sum(attention_full * weight_grad, axis=-1, keepdims=True)
    score_grad = (attention_full * (weight_grad - centre_grad)).astype(jnp.bfloat16)
    query_grad = (
        jnp.einsum("bhqk,bkhd->bqhd", score_grad, key_rows, preferred_element_type=jnp.float32)
        * head_scale
    )
    key_grad = (
        jnp.einsum("bhqk,bqhd->bkhd", score_grad, queries, preferred_element_type=jnp.float32)
        * head_scale
    )
    value_grad = jnp.einsum(
        "bhqk,bqhd->bkhd", attention_low, mixed_grad, preferred_element_type=jnp.float32
    )
    projected_grad = (
        jnp.stack([query_grad, key_grad, value_grad], axis=2)
        .reshape(token_count, 3 * width)
        .astype(jnp.bfloat16)
    )
    joint_shift_grad = jnp.stack(
        [
            jnp.sum(projected_grad[:, :width].astype(jnp.float32), axis=0),
            jnp.sum(projected_grad[:, 2 * width :].astype(jnp.float32), axis=0),
        ]
    )
    joint_grad = contract_first(normed_one, projected_grad)
    first_grad = contract_last(projected_grad, joint_full)
    gain_one_grad = jnp.sum(first_grad * unit_one, axis=0)
    shift_one_grad = jnp.sum(first_grad, axis=0)
    input_grad = residual_grad + norm_back(first_grad, unit_one, factor_one, gain_one)
    group_sums = (
        lax.psum_scatter(
            gain_one_grad.astype(jnp.bfloat16), "shard", scatter_dimension=0, tiled=True
        ).astype(jnp.float32),
        lax.psum_scatter(
            shift_one_grad.astype(jnp.bfloat16), "shard", scatter_dimension=0, tiled=True
        ).astype(jnp.float32),
        lax.psum_scatter(
            joint_grad.astype(jnp.bfloat16), "shard", scatter_dimension=0, tiled=True
        ).astype(jnp.float32),
        lax.psum_scatter(
            joint_shift_grad.astype(jnp.bfloat16), "shard", scatter_dimension=1, tiled=True
        ).astype(jnp.float32),
        lax.psum_scatter(
            mixer_grad.astype(jnp.bfloat16), "shard", scatter_dimension=0, tiled=True
        ).astype(jnp.float32),
        lax.psum_scatter(
            mixer_shift_grad.astype(jnp.bfloat16), "shard", scatter_dimension=0, tiled=True
        ).astype(jnp.float32),
        lax.psum_scatter(
            gain_two_grad.astype(jnp.bfloat16), "shard", scatter_dimension=0, tiled=True
        ).astype(jnp.float32),
        lax.psum_scatter(
            shift_two_grad.astype(jnp.bfloat16), "shard", scatter_dimension=0, tiled=True
        ).astype(jnp.float32),
        lax.psum_scatter(
            router_grad.astype(jnp.bfloat16), "shard", scatter_dimension=0, tiled=True
        ).astype(jnp.float32),
        lax.psum_scatter(
            down_shift_grad.astype(jnp.bfloat16), "shard", scatter_dimension=1, tiled=True
        ).astype(jnp.float32),
    )
    (
        gain_one_grad,
        shift_one_grad,
        joint_grad,
        joint_shift_grad,
        mixer_grad,
        mixer_shift_grad,
        gain_two_grad,
        shift_two_grad,
        router_grad,
        down_shift_grad,
    ) = group_sums
    totals = (
        lax.psum(gain_one_grad.astype(jnp.bfloat16), "rep").astype(jnp.float32),
        lax.psum(shift_one_grad.astype(jnp.bfloat16), "rep").astype(jnp.float32),
        lax.psum(joint_grad.astype(jnp.bfloat16), "rep").astype(jnp.float32),
        lax.psum(joint_shift_grad.astype(jnp.bfloat16), "rep").astype(jnp.float32),
        lax.psum(mixer_grad.astype(jnp.bfloat16), "rep").astype(jnp.float32),
        lax.psum(mixer_shift_grad.astype(jnp.bfloat16), "rep").astype(jnp.float32),
        lax.psum(gain_two_grad.astype(jnp.bfloat16), "rep").astype(jnp.float32),
        lax.psum(shift_two_grad.astype(jnp.bfloat16), "rep").astype(jnp.float32),
        lax.psum(router_grad.astype(jnp.bfloat16), "rep").astype(jnp.float32),
        lax.psum(up_grad.astype(jnp.bfloat16), "rep").astype(jnp.float32),
        lax.psum(up_shift_grad.astype(jnp.bfloat16), "rep").astype(jnp.float32),
        lax.psum(down_grad.astype(jnp.bfloat16), "rep").astype(jnp.float32),
        lax.psum(down_shift_grad.astype(jnp.bfloat16), "rep").astype(jnp.float32),
    )
    return (
        block_out,
        input_grad,
        totals[0],
        totals[1],
        totals[2],
        totals[3],
        totals[4],
        totals[5],
        totals[6],
        totals[7],
        totals[8],
        totals[9],
        totals[10],
        totals[11],
        totals[12],
    )


def solution(mesh):
    placed = (
        P(("shard", "rep"), None),
        P(("shard", "rep"), None),
        P("shard"),
        P("shard"),
        P("shard", None),
        P(None, "shard"),
        P("shard", None),
        P("shard"),
        P("shard"),
        P("shard"),
        P("shard", None),
        P(None, None, "shard"),
        P(None, "shard"),
        P(None, "shard", None),
        P(None, "shard"),
        P(("shard", "rep"), None),
    )
    return jax.shard_map(
        shards,
        mesh=mesh,
        in_specs=placed,
        out_specs=(
            P(("shard", "rep"), None),
            P(("shard", "rep"), None),
            P("shard"),
            P("shard"),
            P("shard", None),
            P(None, "shard"),
            P("shard", None),
            P("shard"),
            P("shard"),
            P("shard"),
            P("shard", None),
            P(None, None, "shard"),
            P(None, "shard"),
            P(None, "shard", None),
            P(None, "shard"),
        ),
        check_vma=False,
    )
```

profile of v0, /device:TPU:0, one launch (start us, length us, event | category | flops | bytes accessed | tf_op | source)
XLA Modules:
  0.0 2104.6 jit_solution(18119825212157746471)
XLA Ops:
  16.2 40.6 %all-reduce.14 = (bf16[768]{0:T(1024)(128)(2,1)S(1)}, bf16[768]{0:T(1024)(128)(2,1)S(1)}, bf16[768]{0:T(1024)(128)(2,1)S(1)}, bf16[768]{0:T(1024)(128)(2,1)S(1)}, bf16[768]{0:T(1024)(128)(2,1)S(1)}) all-reduce(bf16[768]{0:T(1024)(128)(2,1)S(1)} %dynamic-update-slice.1, ...), channel_id=1, replica_groups=mesh['shard'=8,'rep'=4] {'shard'}, use_global_device_ids=true, to_apply=%add.4 | all-reduce | flops 3840 | bytes 15360
  77.2 18.5 all-gather.1
  96.4 31.0 %all_gather.53 = bf16[4,3072]{1,0:T(4,128)(2,1)S(1)} all-gather(bf16[4,384]{1,0:T(4,128)(2,1)} %param.28), channel_id=1, replica_groups=mesh['shard'=8,'rep'=4] {'shard'}, dimensions={1}, use_global_device_ids=true | all-gather | bytes 27648 | tf_op jit(solution)/shard_map/all_gather | solution.py:156
  267.2 215.7 %all-gather.12.cloned.1.call-done = bf16[4,768,3072]{2,1,0:T(8,128)(2,1)} async-done(((bf16[4,768,384]{2,1,0:T(8,128)(2,1)}), bf16[4,768,3072]{2,1,0:T(8,128)(2,1)}) %all-gather.12.cloned.1.call-update) | async-done | bytes 18874384 | tf_op jit(solution)/shard_map/all_gather | solution.py:155
  482.9 29.5 %fusion.17 = (u8[616,3072]{1,0:T(8,128)(4,1)S(1)}, u8[616,3072]{1,0:T(8,128)(4,1)}, f32[4,616,3072]{2,1,0:T(8,128)}) fusion(f32[4,3072]{1,0:T(4,128)S(1)} %copy-done.24, bf16[4,616,768]{2,1,0:T(8,128)(2,1)} %bitcast.130, bf16[4,768,3072]{2,1,0:T(8,128)(2,1)} %all-gather.12.cloned.1.call-done), kind=kOutput, calls=%fused_computation.46 | convolution fusion | flops 11728797696 | bytes 56770560 | tf_op jit(solution)/shard_map/ecd,edf->ecf/dot_general | solution.py:160
  512.4 334.3 %all-gather.14.cloned.1.call-done = bf16[4,3072,768]{2,1,0:T(8,128)(2,1)} async-done(((bf16[4,384,768]{2,1,0:T(8,128)(2,1)}), bf16[4,3072,768]{2,1,0:T(8,128)(2,1)}) %all-gather.14.cloned.1.call-update) | async-done | bytes 18874384 | tf_op jit(solution)/shard_map/all_gather | solution.py:157
  846.7 30.1 %fusion.54 = (bf16[4,3072]{1,0:T(4,128)(2,1)}, bf16[4,616,3072]{2,1,0:T(8,128)(2,1)}) fusion(f32[4,616,3072]{2,1,0:T(8,128)} %get-tuple-element.72, f32[4,3072]{1,0:T(4,128)S(1)} %copy-done.24, bf16[4,616,768]{2,1,0:T(8,128)(2,1)} %get-tuple-element.55, bf16[4,3072,768]{2,1,0:T(8,128)(2,1)} %all-gather.14.cloned.1.call-done), kind=kOutput, calls=%fused_computation.148 | convolution fusion | flops 11717431296 | bytes 68149248 | tf_op jit(solution)/shard_map/ecd,efd->ecf/dot_general | solution.py:191
  876.8 23.7 %convolution_convert_fusion.1 = bf16[4,768,3072]{2,1,0:T(8,128)(2,1)} fusion(bf16[4,616,768]{2,1,0:T(8,128)(2,1)S(1)} %bitcast.131, bf16[4,616,3072]{2,1,0:T(8,128)(2,1)} %get-tuple-element.78), kind=kOutput, calls=%fused_computation.41 | convolution fusion | flops 11636047872 | bytes 37797888 | tf_op jit(solution)/shard_map/ecd,ecf->edf/dot_general | solution.py:198
  900.5 29.5 %copy.152 = bf16[4,768,3072]{1,0,2:T(4,128)(2,1)} copy(bf16[4,768,3072]{2,1,0:T(8,128)(2,1)} %convolution_convert_fusion.1) | data formatting | bytes 37748736
  930.0 20.0 copy.167
  950.7 20.0 all-gather.2
  970.8 20.4 fusion.55
  1024.6 71.8 %fusion.2 = bf16[4,616,3072]{2,1,0:T(8,128)(2,1)} fusion(f32[4,616,3072]{2,1,0:T(8,128)} %get-tuple-element.72, f32[4,3072]{1,0:T(4,128)S(1)} %copy-done.24, u8[616,3072]{1,0:T(8,128)(4,1)} %get-tuple-element.16, u8[616,3072]{1,0:T(8,128)(4,1)S(1)} %get-tuple-element.15), kind=kLoop, calls=%fused_computation.10 | loop fusion | flops 537427968 | bytes 49250304 | tf_op jit(solution)/shard_map/convert_element_type | solution.py:163
  1096.4 20.8 broadcast_add_fusion
  1138.9 17.2 multiply_reduce_fusion.2
  1251.2 21.8 %convolution_convert_fusion = bf16[4,3072,768]{2,1,0:T(8,128)(2,1)} fusion(bf16[4,616,3072]{2,1,0:T(8,128)(2,1)} %fusion.2, bf16[4,616,768]{2,1,0:T(8,128)(2,1)} %get-tuple-element.55), kind=kOutput, calls=%fused_computation.40 | convolution fusion | flops 11636047872 | bytes 37797888 | tf_op jit(solution)/shard_map/ecf,ecd->efd/dot_general | solution.py:202
  1293.1 34.1 %reduce-scatter.21.cloned.1.call-done = bf16[96,768]{1,0:T(8,128)(2,1)} async-done(((bf16[768,768]{1,0:T(8,128)(2,1)}), bf16[96,768]{1,0:T(8,128)(2,1)}) %reduce-scatter.21.cloned.1.call-update) | async-done | bytes 147472 | tf_op jit(solution)/shard_map/reduce_scatter | solution.py:284
  1327.2 82.1 %reduce-scatter.19.cloned.1.call-done = bf16[96,2304]{1,0:T(8,128)(2,1)} async-done(((bf16[768,2304]{1,0:T(8,128)(2,1)}), bf16[96,2304]{1,0:T(8,128)(2,1)}) %reduce-scatter.19.cloned.1.call-update) | async-done | bytes 442384 | tf_op jit(solution)/shard_map/reduce_scatter | solution.py:278
  1409.3 313.2 %reduce-scatter.23.cloned.1.call-done = bf16[4,384,768]{2,1,0:T(8,128)(2,1)} async-done(((bf16[4,3072,768]{2,1,0:T(8,128)(2,1)}), bf16[4,384,768]{2,1,0:T(8,128)(2,1)}) %reduce-scatter.23.cloned.1.call-update) | async-done | bytes 2359312 | tf_op jit(solution)/shard_map/reduce_scatter | solution.py:210
  1723.2 63.7 %reduce-scatter.33.cloned.1.call-done = bf16[96,4]{1,0:T(8,128)(2,1)} async-done(((bf16[768,4]{1,0:T(8,128)(2,1)}), bf16[96,4]{1,0:T(8,128)(2,1)}) %reduce-scatter.33.cloned.1.call-update) | async-done | bytes 784
  1797.5 35.2 %all-reduce.13 = (bf16[768]{0:T(1024)(128)(2,1)S(1)}, bf16[768]{0:T(1024)(128)(2,1)S(1)}, bf16[768]{0:T(1024)(128)(2,1)S(1)}, bf16[768]{0:T(1024)(128)(2,1)S(1)}, bf16[768]{0:T(1024)(128)(2,1)S(1)}) all-reduce(bf16[768]{0:T(1024)(128)(2,1)S(1)} %get-tuple-element.19, ...), channel_id=2, replica_groups=mesh['shard'=8,'rep'=4] {'shard'}, use_global_device_ids=true, to_apply=%region_24.25.clone | all-reduce | flops 3840 | bytes 15360
  1852.5 63.5 %reduce-scatter.27.cloned.1.call-done = bf16[96,4]{1,0:T(8,128)(2,1)} async-done(((bf16[768,4]{1,0:T(8,128)(2,1)}), bf16[96,4]{1,0:T(8,128)(2,1)}) %reduce-scatter.27.cloned.1.call-update) | async-done | bytes 784
  1916.8 65.2 %reduce-scatter.31.cloned.1.call-done = bf16[384,4]{1,0:T(8,128)(2,1)} async-done(((bf16[3072,4]{1,0:T(8,128)(2,1)}), bf16[384,4]{1,0:T(8,128)(2,1)}) %reduce-scatter.31.cloned.1.call-update) | async-done | bytes 3088
  1993.6 93.7 %all-reduce.19.cloned.1.call-done = (bf16[96,2304]{1,0:T(8,128)(2,1)}, bf16[96,768]{1,0:T(8,128)(2,1)}, bf16[4,768,384]{2,1,0:T(8,128)(2,1)}, bf16[4,384,768]{2,1,0:T(8,128)(2,1)}) async-done(((bf16[96,2304]{1,0:T(8,128)(2,1)}, bf16[96,768]{1,0:T(8,128)(2,1)}, bf16[4,768,384]{2,1,0:T(8,128)(2,1)}, bf16[4,384,768]{2,1,0:T(8,128)(2,1)}), (bf16[96,2304]{1,0:T(8,128)(2,1)}, bf16[96,768]{1,0:T(8,128)(2,1)}, ...) | async-done | bytes 5308432 | tf_op jit(solution)/shard_map/psum | solution.py:318
  (284 shorter events, 392.8 us)
Async XLA Ops:
  7.2 130.1 %copy-start.7 = (f32[985,768]{1,0:T(8,128)S(1)}, f32[985,768]{1,0:T(8,128)}, u32[]{:S(2)}) copy-start(f32[985,768]{1,0:T(8,128)} %param.16) | copy-start | bytes 9077764
  7.2 153.7 %all-gather.8.cloned.1.call-start = ((), (), s32[]{:S(2)}) async-start(), calls=%async_computation.8 | async-start | bytes 3981312 | tf_op jit(solution)/shard_map/all_gather | solution.py:89
  7.9 223.7 %all-gather.10.cloned.1.call-start = ((), (), s32[]{:S(2)}) async-start(), calls=%async_computation.9 | async-start | bytes 1327104 | tf_op jit(solution)/shard_map/all_gather | solution.py:91
  8.7 474.2 %all-gather.12.cloned.1.call-start = ((), (), s32[]{:S(2)}) async-start(), calls=%async_computation.10 | async-start | bytes 21233664 | tf_op jit(solution)/shard_map/all_gather | solution.py:155
  9.4 837.3 %all-gather.14.cloned.1.call-start = ((), (), s32[]{:S(2)}) async-start(), calls=%async_computation.11 | async-start | bytes 21233664 | tf_op jit(solution)/shard_map/all_gather | solution.py:157
  10.0 1272.2 %reduce-scatter.29.cloned.1.call-start = ((), (), s32[]{:S(2)}) async-start(), calls=%async_computation.17 | async-start | bytes 21233664
  237.2 16.0 copy-start.11
  261.7 221.2 %copy-start.24 = (f32[4,3072]{1,0:T(4,128)S(1)}, f32[4,3072]{1,0:T(4,128)}, u32[]{:S(2)}) copy-start(f32[4,3072]{1,0:T(4,128)} %convert_element_type.196) | copy-start | bytes 147460
  846.7 30.1 %copy-start.19 = (bf16[2464,768]{1,0:T(8,128)(2,1)S(1)}, bf16[2464,768]{1,0:T(8,128)(2,1)}, u32[]{:S(2)}) copy-start(bf16[2464,768]{1,0:T(8,128)(2,1)} %gather_fusion) | copy-start | bytes 11354116
  950.0 20.7 copy-start.40
  950.0 377.1 %reduce-scatter.21.cloned.1.call-start = ((), (), s32[]{:S(2)}) async-start(), calls=%async_computation.13 | async-start | bytes 1327104 | tf_op jit(solution)/shard_map/reduce_scatter | solution.py:284
  1138.9 20.7 copy-start.3
  1206.7 202.6 %reduce-scatter.19.cloned.1.call-start = ((), (), s32[]{:S(2)}) async-start(), calls=%async_computation.12 | async-start | bytes 3981312 | tf_op jit(solution)/shard_map/reduce_scatter | solution.py:278
  1228.4 14.0 copy-start.9
  1228.4 14.0 copy-start.37
  1228.4 14.0 copy-start.45
  1228.4 14.0 copy-start.47
  1228.4 14.0 copy-start.50
  1250.9 471.6 %reduce-scatter.23.cloned.1.call-start = ((), (), s32[]{:S(2)}) async-start(), calls=%async_computation.14 | async-start | bytes 21233664 | tf_op jit(solution)/shard_map/reduce_scatter | solution.py:210
  1273.0 513.9 %reduce-scatter.33.cloned.1.call-start = ((), (), s32[]{:S(2)}) async-start(), calls=%async_computation.19 | async-start | bytes 221184
  1274.5 577.1 %reduce-scatter.25.cloned.1.call-start = ((), (), s32[]{:S(2)}) async-start(), calls=%async_computation.15 | async-start | bytes 221184
  1277.9 638.1 %reduce-scatter.27.cloned.1.call-start = ((), (), s32[]{:S(2)}) async-start(), calls=%async_computation.16 | async-start | bytes 221184
  1280.5 701.5 %reduce-scatter.31.cloned.1.call-start = ((), (), s32[]{:S(2)}) async-start(), calls=%async_computation.18 | async-start | bytes 884736
  1281.8 805.5 %all-reduce.19.cloned.1.call-start = ((), (), s32[]{:S(2)}) async-start(), calls=%async_computation.20 | async-start | bytes 10616832 | tf_op jit(solution)/shard_map/psum | solution.py:318
  (43 other events, 217.6 us)
Sparse Core Ops, SparseCore 0:
  10.2 67.7 all-gather.7
  80.2 40.0 all-gather.9
  121.8 361.0 all-gather.11
  484.3 362.3 all-gather.13
  950.2 309.7 reduce-scatter.28
  1263.2 63.9 reduce-scatter.20
  1330.8 78.4 reduce-scatter.18
  1413.1 309.3 reduce-scatter.22
  1725.7 61.0 reduce-scatter.32
  1790.6 61.0 reduce-scatter.24
  1854.9 61.0 reduce-scatter.26
  1919.7 62.2 reduce-scatter.30
  1984.6 102.6 all-reduce.18
where the time goes:
time: 2110 us; the launch traced here: 2100 us
  waiting for transfers between devices  1280 us (61%)
  local copies, waits for them, and re-layouts  262 us (12%)
  matrix products  221 us (10%)
  blocking collectives  168 us (8%)
  other arithmetic  154 us (7%)
    all_gather x1, waiting for transfers between devices, shards(): lax.all_gather(expert_down, 'shard', axis=1, tiled=True)  334 us
    reduce_scatter x1, waiting for transfers between devices, shards(): lax.psum_scatter(down_grad.astype(jnp.bfloat16), 'shard', scatter_dimensi...  313 us
    all_gather x1, waiting for transfers between devices, shards(): lax.all_gather(expert_up, 'shard', axis=2, tiled=True)  216 us
    unnamed x18, waiting for transfers between devices  209 us
    unnamed x143, local copies, waits for them, and re-layouts  103 us
    psum x1, waiting for transfers between devices, shards(): lax.psum(joint_grad.astype(jnp.bfloat16), 'rep').astype(jnp.float32)  93.7 us
    reduce_scatter x1, waiting for transfers between devices, shards(): lax.psum_scatter(joint_grad.astype(jnp.bfloat16), 'shard', scatter_dimens...  82.1 us
    unnamed x2, blocking collectives  75.8 us
  transfers between devices with their start and end apart: 13, of which 10 were waited for; matrix products, arithmetic and copies ran while one was open for 24% of the time, Pallas kernels for 0%

commit v1 on v0

v1 whole, which is shorter than its diff:
```python
import functools

import jax
import jax.numpy as jnp
from jax import lax
from jax.sharding import PartitionSpec as P

HEADS = 12
HEAD_DIM = 64
SEQ = 197
CAP = 616


epsilon = 1e-06


def layer_norm(values, gain, shift):
    centre = jnp.mean(values, axis=-1, keepdims=True)
    centred = values - centre
    spread = jnp.mean(centred * centred, axis=-1, keepdims=True)
    factor = lax.rsqrt(spread + epsilon)
    unit_rows = centred * factor
    return (unit_rows * gain + shift, unit_rows, factor)


def norm_back(upstream, unit_rows, factor, gain):
    scaled = upstream * gain
    middle = jnp.mean(scaled, axis=-1, keepdims=True)
    along = jnp.mean(scaled * unit_rows, axis=-1, keepdims=True)
    return factor * (scaled - middle - unit_rows * along)


def contract_first(left_rows, right_rows):
    return lax.dot_general(
        left_rows, right_rows, (((0,), (0,)), ((), ())), preferred_element_type=jnp.float32
    )


def contract_last(left_rows, right_rows):
    return lax.dot_general(
        left_rows, right_rows, (((1,), (1,)), ((), ())), preferred_element_type=jnp.float32
    )


def slot_table(routes, experts, capacity):
    token_count = routes.shape[0]
    hits = (routes[:, :, None] == jnp.arange(experts, dtype=jnp.int32)[None, None, :]).any(axis=1)
    rows = lax.broadcasted_iota(jnp.int32, (token_count, token_count), 0)
    columns = lax.broadcasted_iota(jnp.int32, (token_count, token_count), 1)
    earlier = jnp.dot(
        (columns < rows).astype(jnp.bfloat16),
        hits.astype(jnp.bfloat16),
        preferred_element_type=jnp.float32,
    ).astype(jnp.int32)
    slot_of = jnp.where(hits, earlier, -1).T
    return slot_of[:, None, :] == jnp.arange(capacity, dtype=jnp.int32)[None, :, None]


def gather_all(piece):
    return lax.all_gather(piece, ("shard", "rep"), axis=0, tiled=True)


def my_piece(rows, copies):
    count = rows.shape[0] // copies
    return lax.dynamic_slice_in_dim(rows, lax.axis_index("rep") * count, count, axis=0)


def sum_rows(rows):
    return lax.psum_scatter(rows, ("shard", "rep"), scatter_dimension=0, tiled=True)


def share_rows(rows):
    return lax.all_gather(rows, "rep", axis=0, tiled=True)


def shards(
    tokens_in,
    routes,
    first_gain,
    first_shift,
    joint_weight,
    joint_bias,
    mixer_weight,
    mixer_bias,
    second_gain,
    second_shift,
    router_weight,
    expert_up,
    upward_bias,
    expert_down,
    downward_bias,
    out_grad,
    *,
    groups,
    copies,
):
    token_count, width = tokens_in.shape
    experts, _, part = expert_up.shape
    strip = first_gain.shape[0]
    hidden_width = part * groups
    images = token_count // SEQ
    capacity = CAP
    head_scale = HEAD_DIM ** (-0.5)
    low = jnp.bfloat16
    bias_columns = experts * part // strip

    packed = jnp.concatenate(
        [
            joint_weight,
            mixer_weight,
            router_weight,
            first_gain[:, None],
            first_shift[:, None],
            joint_bias.T,
            mixer_bias[:, None],
            second_gain[:, None],
            second_shift[:, None],
            downward_bias.T,
            upward_bias.reshape(strip, bias_columns),
        ],
        axis=1,
    )
    used = packed.shape[1]
    packed_width = -(-used // 128) * 128
    packed = jnp.pad(packed, ((0, 0), (0, packed_width - used)))
    packed = gather_all(my_piece(packed, copies))
    up_full = gather_all(my_piece(expert_up.reshape(experts * width, part), copies))
    up_full = up_full.reshape(groups, experts, width, part).transpose(1, 2, 0, 3)
    up_full = up_full.reshape(experts, width, hidden_width)
    down_full = gather_all(my_piece(expert_down.reshape(experts * part, width), copies))
    down_full = down_full.reshape(groups, experts, part, width).transpose(1, 0, 2, 3)
    down_full = down_full.reshape(experts, hidden_width, width)

    joint_full = packed[:, : 3 * width]
    mixer_full = packed[:, 3 * width : 4 * width]
    tail = packed[:, 4 * width :]
    router_full = tail[:, :experts]
    vectors = tail[:, experts : experts + 7].astype(jnp.float32).T
    gain_one, shift_one, shift_query, shift_value, mixer_shift, gain_two, shift_two = [
        vectors[i] for i in range(7)
    ]
    down_shift = tail[:, experts + 7 : 2 * experts + 7].astype(jnp.float32).T
    up_shift = (
        tail[:, 2 * experts + 7 : 2 * experts + 7 + bias_columns]
        .reshape(groups, experts, part)
        .transpose(1, 0, 2)
        .reshape(experts, hidden_width)
        .astype(jnp.float32)
    )
    normed_one, unit_one, factor_one = layer_norm(tokens_in, gain_one, shift_one)
    normed_one = normed_one.astype(low)
    shift_all = jnp.concatenate([shift_query, jnp.zeros((width,), jnp.float32), shift_value])
    projected = (
        jnp.dot(normed_one, joint_full, preferred_element_type=jnp.float32) + shift_all
    ).astype(low)
    parted = projected.reshape(images, SEQ, 3, HEADS, HEAD_DIM)
    queries = parted[:, :, 0]
    key_rows = parted[:, :, 1]
    value_rows = parted[:, :, 2]
    scores = (
        jnp.einsum("bqhd,bkhd->bhqk", queries, key_rows, preferred_element_type=jnp.float32)
        * head_scale
    )
    highest_score = jnp.max(scores, axis=-1, keepdims=True)
    log_total = highest_score + jnp.log(
        jnp.sum(jnp.exp(scores - highest_score), axis=-1, keepdims=True)
    )
    attention = jnp.exp(scores - log_total).astype(low)
    mixed = jnp.einsum("bhqk,bkhd->bqhd", attention, value_rows, preferred_element_type=jnp.float32)
    mixed = mixed.reshape(token_count, width).astype(low)
    residual_one = tokens_in + (
        jnp.dot(mixed, mixer_full, preferred_element_type=jnp.float32) + mixer_shift
    )
    normed_two, unit_two, factor_two = layer_norm(residual_one, gain_two, shift_two)
    normed_two = normed_two.astype(low)
    logits = jnp.dot(normed_two, router_full, preferred_element_type=jnp.float32)
    router_probs = jax.nn.softmax(logits, axis=-1)

    seated = slot_table(routes, experts, capacity)
    seats = seated.astype(low)
    flat_seats = seats.reshape(experts * capacity, token_count)
    gate_slots = jnp.sum(jnp.where(seated, router_probs.T[:, None, :], 0.0), axis=-1)[:, :, None]
    dispatched = (
        jnp.dot(flat_seats, normed_two, preferred_element_type=jnp.float32)
        .astype(low)
        .reshape(experts, capacity, width)
    )
    grad_slots = jnp.dot(
        flat_seats, out_grad.astype(low), preferred_element_type=jnp.float32
    ).reshape(experts, capacity, width)
    result_grad = (gate_slots * grad_slots).astype(low)

    hidden = (
        jnp.einsum("ecd,edf->ecf", dispatched, up_full, preferred_element_type=jnp.float32)
        + up_shift[:, None, :]
    )
    normal_cdf = 0.5 * (1.0 + lax.erf(hidden * 0.7071067811865476))
    active = (hidden * normal_cdf).astype(low)
    density = jnp.exp(-0.5 * hidden * hidden) * 0.3989422804014327
    active_grad = jnp.einsum(
        "ecd,efd->ecf", result_grad, down_full, preferred_element_type=jnp.float32
    )
    hidden_grad = (active_grad * (normal_cdf + hidden * density)).astype(low)
    up_grad = jnp.einsum(
        "ecd,ecf->edf", dispatched, hidden_grad, preferred_element_type=jnp.float32
    ).astype(low)
    up_grad = up_grad.reshape(experts, width, groups, part).transpose(2, 0, 1, 3)
    up_grad = sum_rows(up_grad.reshape(groups * experts * width, part))
    down_grad = jnp.einsum(
        "ecf,ecd->efd", active, result_grad, preferred_element_type=jnp.float32
    ).astype(low)
    down_grad = down_grad.reshape(experts, groups, part, width).transpose(1, 0, 2, 3)
    down_grad = sum_rows(down_grad.reshape(groups * experts * part, width))
    up_grad = share_rows(up_grad).astype(jnp.float32).reshape(experts, width, part)
    down_grad = share_rows(down_grad).astype(jnp.float32).reshape(experts, part, width)

    expert_result = (
        jnp.einsum("ecf,efd->ecd", active, down_full, preferred_element_type=jnp.float32)
        + down_shift[:, None, :]
    )
    gate_grad = jnp.sum(grad_slots * expert_result, axis=-1)
    weighted = (gate_slots * expert_result).astype(low).reshape(experts * capacity, width)
    block_out = residual_one + contract_first(flat_seats, weighted)
    probs_grad = jnp.sum(jnp.where(seated, gate_grad[:, :, None], 0.0), axis=1).T
    logit_grad = (
        router_probs * (probs_grad - jnp.sum(router_probs * probs_grad, axis=-1, keepdims=True))
    ).astype(low)
    router_grad = contract_first(normed_two, logit_grad)
    down_shift_grad = jnp.sum(result_grad.astype(jnp.float32), axis=1)
    up_shift_grad = jnp.sum(hidden_grad.astype(jnp.float32), axis=1)
    dispatched_grad = jnp.einsum(
        "ecf,edf->ecd", hidden_grad, up_full, preferred_element_type=jnp.float32
    )
    normed_grad = contract_last(logit_grad, router_full) + contract_first(
        flat_seats, dispatched_grad.astype(low).reshape(experts * capacity, width)
    )
    gain_two_grad = jnp.sum(normed_grad * unit_two, axis=0)
    shift_two_grad = jnp.sum(normed_grad, axis=0)
    residual_grad = out_grad + norm_back(normed_grad, unit_two, factor_two, gain_two)
    mixer_in_grad = residual_grad.astype(low)
    mixer_shift_grad = jnp.sum(mixer_in_grad.astype(jnp.float32), axis=0)
    mixer_grad = contract_first(mixed, mixer_in_grad)
    mixed_grad = (
        contract_last(mixer_in_grad, mixer_full)
        .astype(low)
        .reshape(images, SEQ, HEADS, HEAD_DIM)
    )
    scores_again = (
        jnp.einsum("bqhd,bkhd->bhqk", queries, key_rows, preferred_element_type=jnp.float32)
        * head_scale
    )
    attention_full = jnp.exp(scores_again - log_total)
    attention_low = attention_full.astype(low)
    weight_grad = jnp.einsum(
        "bqhd,bkhd->bhqk", mixed_grad, value_rows, preferred_element_type=jnp.float32
    )
    centre_grad = jnp.sum(attention_full * weight_grad, axis=-1, keepdims=True)
    score_grad = (attention_full * (weight_grad - centre_grad)).astype(low)
    query_grad = (
        jnp.einsum("bhqk,bkhd->bqhd", score_grad, key_rows, preferred_element_type=jnp.float32)
        * head_scale
    ).astype(low)
    key_grad = (
        jnp.einsum("bhqk,bqhd->bkhd", score_grad, queries, preferred_element_type=jnp.float32)
        * head_scale
    ).astype(low)
    value_grad = jnp.einsum(
        "bhqk,bqhd->bkhd", attention_low, mixed_grad, preferred_element_type=jnp.float32
    ).astype(low)
    projected_grad = jnp.concatenate(
        [
            query_grad.reshape(token_count, width),
            key_grad.reshape(token_count, width),
            value_grad.reshape(token_count, width),
        ],
        axis=1,
    )
    joint_sums = jnp.sum(projected_grad.astype(jnp.float32), axis=0)
    joint_grad = contract_first(normed_one, projected_grad)
    first_grad = contract_last(projected_grad, joint_full)
    gain_one_grad = jnp.sum(first_grad * unit_one, axis=0)
    shift_one_grad = jnp.sum(first_grad, axis=0)
    input_grad = residual_grad + norm_back(first_grad, unit_one, factor_one, gain_one)

    small = jnp.stack(
        [
            gain_one_grad,
            shift_one_grad,
            joint_sums[:width],
            joint_sums[2 * width :],
            mixer_shift_grad,
            gain_two_grad,
            shift_two_grad,
        ],
        axis=1,
    )
    packed_grad = jnp.concatenate(
        [
            joint_grad.astype(low),
            mixer_grad.astype(low),
            router_grad.astype(low),
            small.astype(low),
            down_shift_grad.T.astype(low),
            up_shift_grad.astype(low)
            .reshape(experts, groups, part)
            .transpose(1, 0, 2)
            .reshape(groups * strip, bias_columns),
        ],
        axis=1,
    )
    packed_grad = jnp.pad(packed_grad, ((0, 0), (0, packed_width - used)))
    packed_grad = share_rows(sum_rows(packed_grad)).astype(jnp.float32)
    end = packed_grad[:, 4 * width :]
    line = end[:, experts : experts + 7].T
    return (
        block_out,
        input_grad,
        line[0],
        line[1],
        packed_grad[:, : 3 * width],
        line[2:4],
        packed_grad[:, 3 * width : 4 * width],
        line[4],
        line[5],
        line[6],
        end[:, :experts],
        up_grad,
        end[:, 2 * experts + 7 : 2 * experts + 7 + bias_columns].reshape(experts, part),
        down_grad,
        end[:, experts + 7 : 2 * experts + 7].T,
    )


def solution(mesh):
    placed = (
        P(("shard", "rep"), None),
        P(("shard", "rep"), None),
        P("shard"),
        P("shard"),
        P("shard", None),
        P(None, "shard"),
        P("shard", None),
        P("shard"),
        P("shard"),
        P("shard"),
        P("shard", None),
        P(None, None, "shard"),
        P(None, "shard"),
        P(None, "shard", None),
        P(None, "shard"),
        P(("shard", "rep"), None),
    )
    return jax.shard_map(
        functools.partial(
            shards, groups=mesh.shape["shard"], copies=mesh.shape["rep"]
        ),
        mesh=mesh,
        in_specs=placed,
        out_specs=(
            P(("shard", "rep"), None),
            P(("shard", "rep"), None),
            P("shard"),
            P("shard"),
            P("shard", None),
            P(None, "shard"),
            P("shard", None),
            P("shard"),
            P("shard"),
            P("shard"),
            P("shard", None),
            P(None, None, "shard"),
            P(None, "shard"),
            P(None, "shard", None),
            P(None, "shard"),
        ),
        check_vma=False,
    )
```

time: 2110 us -> 1050 us (0.50)
  waiting for transfers between devices: 1280 us -> 504 us
  blocking collectives: 168 us -> 7.85 us
  other arithmetic: 154 us -> 44 us
  local copies, waits for them, and re-layouts: 262 us -> 214 us
  matrix products: 221 us -> 255 us
    all_gather x4 -> x5, waiting for transfers between devices: 550 us -> 232 us  [the longest x3 199 us: gather_all(): return lax.all_gather(piece, ('shard', 'rep'), axis=0, tiled=True)]
    reduce_scatter x3 -> x2, waiting for transfers between devices: 429 us -> 182 us  [sum_rows(): lax.psum_scatter(rows, ('shard', 'rep'), scatter_dimension=0, tiled=True)]
    unnamed x18 -> x9, waiting for transfers between devices: 209 us -> 90.7 us
    psum x1 -> x0, waiting for transfers between devices: 93.7 us -> none  [shards(): lax.psum(joint_grad.astype(jnp.bfloat16), 'rep').astype(jnp.float32)]
    convert_element_type x24 -> x4, other arithmetic: 98.1 us -> 8.63 us  [the longest x1 6.95 us: shards(): score_grad = (attention_full * (weight_grad - centre_grad)).astype(low)]
    all_gather x4 -> x1, blocking collectives: 86.2 us -> 7.85 us  [share_rows(): return lax.all_gather(rows, 'rep', axis=0, tiled=True)]
    unnamed x2 -> x0, blocking collectives: 75.8 us -> none
    unnamed x143 -> x133, local copies, waits for them, and re-layouts: 103 us -> 31 us
  transfers between devices with their start and end apart: 13 -> 8, of which waited for: 10 -> 7; matrix products, arithmetic and copies ran while one was open for 24% -> 36% of each run, Pallas kernels for 0% -> 0%
where the time goes in v1:
time: 1050 us; the launch traced here: 1040 us
  waiting for transfers between devices  504 us (48%)
  matrix products  255 us (24%)
  local copies, waits for them, and re-layouts  214 us (20%)
  other arithmetic  44 us (4%)
  between operations  15.5 us (1%)
    all_gather x3, waiting for transfers between devices, gather_all(): return lax.all_gather(piece, ('shard', 'rep'), axis=0, tiled=True)  199 us
    reduce_scatter x2, waiting for transfers between devices, sum_rows(): lax.psum_scatter(rows, ('shard', 'rep'), scatter_dimension=0, tiled=True)  182 us
    unnamed x9, waiting for transfers between devices  90.7 us
    dot_general x5, matrix products, contract_first(): lax.dot_general(left_rows, right_rows, (((0,), (0,)), ((), ())), preferre...  49.7 us
    all_gather x2, waiting for transfers between devices, share_rows(): return lax.all_gather(rows, 'rep', axis=0, tiled=True)  32.5 us
    dot_general x1, matrix products, shards(): jnp.einsum('ecd,efd->ecf', result_grad, down_full, preferred_element_type...  32.5 us
    unnamed x133, local copies, waits for them, and re-layouts  31 us
    dot_general x1, matrix products, shards(): jnp.einsum('ecf,ecd->efd', active, result_grad, preferred_element_type=jn...  27.5 us
  transfers between devices with their start and end apart: 8, of which 7 were waited for; matrix products, arithmetic and copies ran while one was open for 36% of the time, Pallas kernels for 0%

profile of v1, /device:TPU:0, one launch (start us, length us, event | category | flops | bytes accessed | tf_op | source)
XLA Modules:
  0.0 1040.3 jit_solution(6565840946167646066)
XLA Ops:
  27.5 56.1 %all-gather.6.cloned.1.call-done = bf16[768,3200]{1,0:T(8,128)(2,1)} async-done(((bf16[24,3200]{1,0:T(8,128)(2,1)}), bf16[768,3200]{1,0:T(8,128)(2,1)}) %all-gather.6.cloned.1.call-update) | async-done | bytes 4915216 | tf_op jit(solution)/shard_map/all_gather | solution.py:60
  88.5 9.0 add_convert_fusion
  97.6 14.9 %reshape.220 = bf16[5,197,3,12,64]{4,3,2,1,0:T(8,128)(2,1)} reshape(bf16[985,2304]{1,0:T(8,128)(2,1)} %add_convert_fusion) | data formatting | bytes 9077760 | tf_op jit(solution)/shard_map/reshape | solution.py:156
  112.5 9.8 fusion.61
  173.0 36.3 %all-gather.8.cloned.1.call-done = bf16[24576,384]{1,0:T(8,128)(2,1)} async-done(((bf16[768,384]{1,0:T(8,128)(2,1)}), bf16[24576,384]{1,0:T(8,128)(2,1)}) %all-gather.8.cloned.1.call-update) | async-done | bytes 18874384 | tf_op jit(solution)/shard_map/all_gather | solution.py:60
  209.4 18.6 %copy.233 = bf16[8,4,96,8,384]{4,3,0,2,1:T(8,128)(2,1)} copy(bf16[8,4,96,8,384]{4,3,2,1,0:T(8,128)(2,1)} %bitcast.146) | data formatting | bytes 37748736 | tf_op jit(solution)/shard_map/reshape | solution.py:129
  227.9 106.6 %all-gather.10.cloned.1.call-done = bf16[12288,768]{1,0:T(8,128)(2,1)} async-done(((bf16[384,768]{1,0:T(8,128)(2,1)}), bf16[12288,768]{1,0:T(8,128)(2,1)}) %all-gather.10.cloned.1.call-update) | async-done | bytes 18874384 | tf_op jit(solution)/shard_map/all_gather | solution.py:60
  334.5 20.7 %copy.194 = bf16[4,8,384,768]{3,2,1,0:T(8,128)(2,1)} copy(bf16[4,8,384,768]{3,2,0,1:T(8,128)(2,1)} %bitcast.147) | data formatting | bytes 37748736 | tf_op jit(solution)/shard_map/transpose | solution.py:131
  355.2 21.6 %multiply_convert_fusion = (bf16[4,616,3072]{2,1,0:T(8,128)(2,1)}, f32[4,616,3072]{2,1,0:T(8,128)}) fusion(f32[4,3072]{1,0:T(4,128)S(1)} %bitcast.158, bf16[4,616,768]{2,1,0:T(8,128)(2,1)S(1)} %bitcast.168, bf16[4,768,3072]{2,1,0:T(8,128)(2,1)S(1)} %bitcast.149), kind=kOutput, calls=%fused_computation.7 | convolution fusion | flops 11672027136 | bytes 68124672 | tf_op jit(solution)/shard_map/ecd,edf->ecf/dot_general | solution.py:194
  376.8 21.8 %fusion.66 = f32[4,616,768]{2,1,0:T(8,128)} fusion(bf16[4,616,3072]{2,1,0:T(8,128)(2,1)} %get-tuple-element.125, bf16[4,3072,768]{2,1,0:T(8,128)(2,1)} %bitcast.150), kind=kOutput, calls=%fused_computation.141 | convolution fusion | flops 11626610688 | bytes 41582592 | tf_op jit(solution)/shard_map/ecf,efd->ecd/dot_general | solution.py:218
  398.5 8.6 multiply_reduce_fusion.2
  410.7 27.5 %convolution_convert_fusion = bf16[4,3072,768]{2,1,0:T(8,128)(2,1)} fusion(bf16[4,616,3072]{2,1,0:T(8,128)(2,1)} %get-tuple-element.125, bf16[4,616,768]{2,1,0:T(8,128)(2,1)S(1)} %get-tuple-element.113), kind=kOutput, calls=%fused_computation.15 | convolution fusion | flops 11636047872 | bytes 37797888 | tf_op jit(solution)/shard_map/ecf,ecd->efd/dot_general | solution.py:209
  438.3 17.1 %copy.216 = bf16[4,8,384,768]{3,2,0,1:T(8,128)(2,1)} copy(bf16[4,8,384,768]{3,2,1,0:T(8,128)(2,1)} %bitcast.152) | data formatting | bytes 37748736 | tf_op jit(solution)/shard_map/reshape | solution.py:212
  455.4 32.5 %fusion.65 = (bf16[4,3072]{1,0:T(4,128)(2,1)S(1)}, bf16[4,616,3072]{2,1,0:T(8,128)(2,1)}) fusion(f32[4,616,3072]{2,1,0:T(8,128)} %get-tuple-element.126, f32[4,3072]{1,0:T(4,128)S(1)} %bitcast.159, bf16[4,616,768]{2,1,0:T(8,128)(2,1)} %copy-done.21, bf16[4,3072,768]{2,1,0:T(8,128)(2,1)} %bitcast.151), kind=kOutput, calls=%fused_computation.140 | convolution fusion | flops 11717431296 | bytes 68149248 | tf_op jit(solution)/shard_map/ecd,efd->ecf/dot_general | solution.py:200
  487.9 25.0 %convolution_convert_fusion.1 = bf16[4,768,3072]{2,1,0:T(8,128)(2,1)} fusion(bf16[4,616,768]{2,1,0:T(8,128)(2,1)S(1)} %bitcast.169, bf16[4,616,3072]{2,1,0:T(8,128)(2,1)} %get-tuple-element.136), kind=kOutput, calls=%fused_computation.16 | convolution fusion | flops 11636047872 | bytes 37797888 | tf_op jit(solution)/shard_map/ecd,ecf->edf/dot_general | solution.py:204
  512.9 19.0 %copy.235 = bf16[4,96,8,8,384]{4,3,1,0,2:T(8,128)(2,1)} copy(bf16[4,96,8,8,384]{4,3,2,1,0:T(8,128)(2,1)} %bitcast.153) | data formatting | bytes 37748736 | tf_op jit(solution)/shard_map/reshape | solution.py:207
  535.3 29.6 %fusion.6 = f32[985,768,1]{1,0,2:T(8,128)} fusion(s32[4,985]{1,0:T(4,128)S(1)} %fusion.42, bf16[4,616,3072]{2,1,0:T(8,128)(2,1)} %get-tuple-element.136, bf16[4,768,3072]{2,1,0:T(8,128)(2,1)} %bitcast.148), kind=kOutput, calls=%fused_computation.21 | convolution fusion | flops 15358863360 | bytes 37054864 | tf_op jit(solution)/shard_map/dot_general | solution.py:34
  652.7 10.8 %multiply_reduce_fusion.4 = (bf16[768]{0:T(1024)(128)(2,1)S(1)}, f32[985]{0:T(1024)S(1)}, f32[985]{0:T(1024)S(1)}, bf16[768]{0:T(1024)(128)(2,1)S(1)}, f32[985,768]{1,0:T(8,128)}) fusion(f32[985,768]{1,0:T(8,128)} %param.16, f32[985]{0:T(1024)S(1)} %copy-done.54, f32[985]{0:T(1024)S(1)} %copy-done.50, f32[768]{0:T(1024)S(1)} %copy-done.52, ...), kind=kOutput, calls=%fused_computation.47 | convolution fusion | flops 3492664576 | bytes 14352784 | tf_op jit(solution)/shard_map/dot_general | solution.py:40
  675.9 9.0 concatenate.16
  691.1 181.8 %reduce-scatter.6.cloned.1.call-done = bf16[768,384]{1,0:T(8,128)(2,1)} async-done(((bf16[24576,384]{1,0:T(8,128)(2,1)}), bf16[768,384]{1,0:T(8,128)(2,1)}) %reduce-scatter.6.cloned.1.call-update) | async-done | bytes 589840 | tf_op jit(solution)/shard_map/reduce_scatter | solution.py:69
  878.7 9.9 bitcast_add_fusion.1
  888.6 89.9 %reduce-scatter.10.cloned.1.call-done = bf16[24,3200]{1,0:T(8,128)(2,1)} async-done(((bf16[768,3200]{1,0:T(8,128)(2,1)}), bf16[24,3200]{1,0:T(8,128)(2,1)}) %reduce-scatter.10.cloned.1.call-update) | async-done | bytes 153616
  991.9 11.3 %all-gather.14.cloned.1.call-done = bf16[1536,768]{1,0:T(8,128)(2,1)} async-done(((bf16[384,768]{1,0:T(8,128)(2,1)}), bf16[1536,768]{1,0:T(8,128)(2,1)}) %all-gather.14.cloned.1.call-update) | async-done | bytes 2359312 | tf_op jit(solution)/shard_map/all_gather | solution.py:73
  1007.6 21.2 %all-gather.12.cloned.1.call-done = bf16[3072,384]{1,0:T(8,128)(2,1)} async-done(((bf16[768,384]{1,0:T(8,128)(2,1)}), bf16[3072,384]{1,0:T(8,128)(2,1)}) %all-gather.12.cloned.1.call-update) | async-done | bytes 2359312 | tf_op jit(solution)/shard_map/all_gather | solution.py:73
  (248 shorter events, 216.2 us)
Async XLA Ops:
  7.2 9.3 copy-start
  7.2 76.4 %all-gather.6.cloned.1.call-start = ((), (), s32[]{:S(2)}) async-start(), calls=%async_computation.3 | async-start | bytes 5068800 | tf_op jit(solution)/shard_map/all_gather | solution.py:60
  16.4 192.9 %all-gather.8.cloned.1.call-start = ((), (), s32[]{:S(2)}) async-start(), calls=%async_computation.4 | async-start | bytes 19464192 | tf_op jit(solution)/shard_map/all_gather | solution.py:60
  17.4 317.1 %all-gather.10.cloned.1.call-start = ((), (), s32[]{:S(2)}) async-start(), calls=%async_computation.5 | async-start | bytes 19464192 | tf_op jit(solution)/shard_map/all_gather | solution.py:60
  19.4 670.9 %reduce-scatter.8.cloned.1.call-start = ((), (), s32[]{:S(2)}) async-start(), calls=%async_computation.8 | async-start | bytes 19464192 | tf_op jit(solution)/shard_map/reduce_scatter | solution.py:69
  25.1 63.5 %copy-start.49 = (f32[985]{0:T(1024)}, f32[985]{0:T(1024)S(1)}, u32[]{:S(2)}) copy-start(f32[985]{0:T(1024)S(1)} %broadcast_multiply_fusion.5) | copy-start | bytes 11824
  27.4 70.1 %copy-start.53 = (f32[985]{0:T(1024)}, f32[985]{0:T(1024)S(1)}, u32[]{:S(2)}) copy-start(f32[985]{0:T(1024)S(1)} %add_rsqrt_fusion.1) | copy-start | bytes 11824
  84.8 313.8 %copy-start.55 = (f32[4,768]{1,0:T(4,128)}, f32[4,768]{1,0:T(4,128)S(1)}, u32[]{:S(2)}) copy-start(f32[4,768]{1,0:T(4,128)S(1)} %copy.195) | copy-start | bytes 36868
  88.5 9.1 copy-start.51
  88.5 75.4 %copy-start.41 = (f32[768]{0:T(1024)}, f32[768]{0:T(1024)S(1)}, u32[]{:S(2)}) copy-start(f32[768]{0:T(1024)S(1)} %get-tuple-element.98) | copy-start | bytes 9220
  334.5 20.7 %copy-start.11 = (bf16[8,4,96,8,384]{4,3,0,2,1:T(8,128)(2,1)S(1)}, bf16[8,4,96,8,384]{4,3,0,2,1:T(8,128)(2,1)}, u32[]{:S(2)}) copy-start(bf16[8,4,96,8,384]{4,3,0,2,1:T(8,128)(2,1)} %copy.233) | copy-start | bytes 56623108
  334.5 20.7 %copy-start.60 = (bf16[2464,768]{1,0:T(8,128)(2,1)S(1)}, bf16[2464,768]{1,0:T(8,128)(2,1)}, u32[]{:S(2)}) copy-start(bf16[2464,768]{1,0:T(8,128)(2,1)} %convolution_convert_fusion.3) | copy-start | bytes 11354116
  410.7 27.5 %copy-start.21 = (bf16[4,616,768]{2,1,0:T(8,128)(2,1)}, bf16[4,616,768]{2,1,0:T(8,128)(2,1)S(1)}, u32[]{:S(2)}) copy-start(bf16[4,616,768]{2,1,0:T(8,128)(2,1)S(1)} %get-tuple-element.113) | copy-start | bytes 11354116
  455.4 417.6 %reduce-scatter.6.cloned.1.call-start = ((), (), s32[]{:S(2)}) async-start(), calls=%async_computation.6 | async-start | bytes 19464192 | tf_op jit(solution)/shard_map/reduce_scatter | solution.py:69
  455.4 32.5 %copy-start.61 = (bf16[2464,768]{1,0:T(8,128)(2,1)S(1)}, bf16[2464,768]{1,0:T(8,128)(2,1)}, u32[]{:S(2)}) copy-start(bf16[2464,768]{1,0:T(8,128)(2,1)} %convolution_convert_fusion.3) | copy-start | bytes 11354116
  531.9 446.6 %reduce-scatter.10.cloned.1.call-start = ((), (), s32[]{:S(2)}) async-start(), calls=%async_computation.10 | async-start | bytes 5068800
  535.3 29.6 %copy-start.38 = (f32[985]{0:T(1024)S(1)}, f32[985]{0:T(1024)}, u32[]{:S(2)}) copy-start(f32[985]{0:T(1024)} %copy-done.37) | copy-start | bytes 11824
  535.3 29.6 %copy-start.42 = (f32[768]{0:T(1024)S(1)}, f32[768]{0:T(1024)}, u32[]{:S(2)}) copy-start(f32[768]{0:T(1024)} %copy-done.41) | copy-start | bytes 9220
  535.3 29.7 %copy-start.44 = (f32[985]{0:T(1024)S(1)}, f32[985]{0:T(1024)}, u32[]{:S(2)}) copy-start(f32[985]{0:T(1024)} %copy-done.43) | copy-start | bytes 11824
  652.7 12.7 %copy-start.18 = (f32[985,768]{1,0:T(8,128)S(1)}, f32[985,768]{1,0:T(8,128)}, u32[]{:S(2)}) copy-start(f32[985,768]{1,0:T(8,128)} %copy-done.17) | copy-start | bytes 9077764
  652.7 12.7 %copy-start.27 = (bf16[985,768]{0,1:T(8,128)(2,1)S(1)}, bf16[985,768]{0,1:T(8,128)(2,1)}, u32[]{:S(2)}) copy-start(bf16[985,768]{0,1:T(8,128)(2,1)} %copy-done.26) | copy-start | bytes 4538884
  690.3 312.9 %all-gather.14.cloned.1.call-start = ((), (), s32[]{:S(2)}) async-start(), calls=%async_computation.9 | async-start | bytes 2949120 | tf_op jit(solution)/shard_map/all_gather | solution.py:73
  691.1 337.8 %all-gather.12.cloned.1.call-start = ((), (), s32[]{:S(2)}) async-start(), calls=%async_computation.7 | async-start | bytes 2949120 | tf_op jit(solution)/shard_map/all_gather | solution.py:73
  1003.2 29.8 %copy-start.1 = (bf16[4,768,384]{2,1,0:T(8,128)(2,1)S(1)}, bf16[4,768,384]{2,1,0:T(8,128)(2,1)}, u32[]{:S(2)}) copy-start(bf16[4,768,384]{2,1,0:T(8,128)(2,1)} %param.27) | copy-start | bytes 7077892
  (46 other events, 229.1 us)
Sparse Core Ops, SparseCore 0:
  16.6 66.9 all-gather.5
  87.1 122.2 all-gather.7
  212.3 122.1 all-gather.9
  455.5 205.1 reduce-scatter.7
  666.9 205.9 reduce-scatter.5
  878.5 99.9 reduce-scatter.9
  980.1 23.0 all-gather.13
  1004.8 24.0 all-gather.11
